TPU v7x, 32 devices: a whole 2x2x4 slice. The times are simulated.
32 devices in a mesh: ex: 8 (over y, x, core), feat: 4 (over z).
Axes of the slice: x: 2, y: 2, z: 4, core: 2. Of those that a mesh axis runs over, the one named last changes fastest.
Arguments:
- activations: bfloat16 [512, 64, 4096], P('ex', None, 'feat'), may hold values from -6 to 6
- output_gradient_rows: bfloat16 [512, 64, 4096], P('ex', None, 'feat'), may hold values from -6 to 6
- adapter_down_matrix: bfloat16 [4096, 128], P('feat'), may hold values from -0.09375 to 0.09375
- rank_side_sketch: bfloat16 [128, 64], replicated, may hold values from -0.5 to 0.5
- output_side_sketch: bfloat16 [4096, 128], P('feat'), may hold values from -0.09375 to 0.09375
- heldout_gradient_features: float32 [256, 8192], P('ex', 'feat'), may hold values from -6 to 6
- heldout_language_permutation: int32 [256], P('ex'), may hold values from 0 to 255, each once
Outputs:
- scores: float32 [512, 64], P('ex')
Inputs may be any that keep to these rules, and one draw needn't show every extreme that they name: `heldout_language_permutation`: every value of 0 to 255 appears once, so every language has 4 validation examples.
All inputs are finite; a program needn't handle non-finite values.
Results may differ from a plain program's by a relative error of at most 0.0029.
Values sent between devices are 32-bit elements; how exact they have to be, the bound alone decides.
No kernel may reach another device: no remote copies, remote signals or barrier semaphores. Data moves between devices by JAX's collectives and lax.ppermute only.
A program may use at most 64 MiB of HBM per device.

v0:
```python
import jax
import jax.numpy as jnp
from jax import lax
from jax.sharding import PartitionSpec as P

KF = 8192
LANGS = 64


def shards(
    activations,
    output_gradient_rows,
    adapter_down_matrix,
    rank_side_sketch,
    output_side_sketch,
    heldout_gradient_features,
    heldout_language_permutation,
):
    highest = lax.Precision.HIGHEST
    ex_dev = activations.shape[0]
    down_projection_name = jnp.dot(
        adapter_down_matrix, rank_side_sketch, preferred_element_type=jnp.float32
    ).astype(jnp.bfloat16)
    rank_part = jnp.einsum(
        "esd,dr->esr", activations, down_projection_name, preferred_element_type=jnp.float32
    )
    rank_side = lax.psum(rank_part, "feat")
    out_part = jnp.einsum(
        "esd,dk->esk", output_gradient_rows, output_side_sketch, preferred_element_type=jnp.float32
    )
    out_side = lax.psum_scatter(out_part, "feat", scatter_dimension=2, tiled=True)
    grad_feat = jnp.einsum("esk,esr->ekr", out_side, rank_side, precision=highest).reshape(
        ex_dev, -1
    )
    val_square = lax.psum(
        jnp.sum(heldout_gradient_features * heldout_gradient_features, axis=1), "feat"
    )
    val_unit = heldout_gradient_features * lax.rsqrt(val_square + 1e-06)[:, None]
    lang = heldout_language_permutation % LANGS
    onehot = (lang[:, None] == jnp.arange(LANGS, dtype=jnp.int32)[None, :]).astype(jnp.float32)
    lang_part = jnp.dot(onehot.T, val_unit, precision=highest)
    lang_mean = lax.psum(lang_part, "ex") / (
        heldout_language_permutation.shape[0] * lax.axis_size("ex") // LANGS
    )
    inner_part = jnp.dot(grad_feat, lang_mean.T, precision=highest)
    square_part = jnp.sum(grad_feat * grad_feat, axis=1)
    inner, squares = lax.psum((inner_part, square_part), "feat")
    per_lang = heldout_language_permutation.shape[0] * lax.axis_size("ex") // LANGS
    scale = jnp.sqrt(jnp.float32(KF * per_lang))
    return scale * inner * lax.rsqrt(squares + 1e-06)[:, None]


def solution(mesh):
    placed = (
        P("ex", None, "feat"),
        P("ex", None, "feat"),
        P("feat", None),
        P(),
        P("feat", None),
        P("ex", "feat"),
        P("ex"),
    )
    return jax.shard_map(
        shards, mesh=mesh, in_specs=placed, out_specs=P("ex", None), check_vma=False
    )
```

profile of v0, /device:TPU:0, one launch (start us, length us, event | category | flops | bytes accessed | tf_op | source)
XLA Modules:
  0.0 268.0 jit_solution(1419638174889042181)
XLA Ops:
  6.5 0.0 copy-start
  6.5 0.0 all-reduce.4.cloned.1.call-start
  6.5 7.4 %convolution_bitcast_fusion = f32[64,64,64]{2,1,0:T(8,128)} fusion(bf16[64,64,1024]{2,1,0:T(8,128)(2,1)} %param.7, bf16[1024,128]{1,0:T(8,128)(2,1)} %param.9, bf16[128,64]{0,1:T(8,128)(2,1)} %param.10), kind=kOutput, calls=%fused_computation | convolution fusion | flops 553713664 | bytes 9715712 | tf_op jit(solution)/shard_map/esd,dr->esr/dot_general | solution.py:24
  14.0 0.0 all-reduce.4.cloned.1.call-update
  14.0 0.0 copy-start.1
  14.0 0.0 copy-start.2
  14.0 0.0 reduce-scatter.2.cloned.1.call-start
  14.1 0.0 copy-done
  14.1 9.5 %fusion.3 = f32[64,64,128]{1,2,0:T(8,128)} fusion(bf16[64,64,1024]{2,1,0:T(8,128)(2,1)} %param.8, bf16[1024,128]{1,0:T(8,128)(2,1)S(1)} %copy-done), kind=kOutput, calls=%fused_computation.6 | convolution fusion | flops 1073741824 | bytes 10747904 | tf_op jit(solution)/shard_map/esd,dk->esk/dot_general | solution.py:28
  23.5 0.0 reduce-scatter.2.cloned.1.call-update
  23.6 0.0 all-reduce.6.cloned.1.call-start
  23.6 0.0 copy-done.1
  23.6 0.1 multiply_reduce_fusion.1
  23.7 14.1 %psum.36 = f32[32]{0:T(128)S(1)} all-reduce(f32[32]{0:T(128)S(1)} %multiply_reduce_fusion.1), channel_id=1, replica_groups=mesh['ex'=8,'feat'=4] {'feat'}, use_global_device_ids=true, to_apply=%region_3.0 | all-reduce | flops 32 | bytes 256 | tf_op jit(solution)/shard_map/psum | solution.py:35
  37.8 0.0 copy-done.2
  37.8 1.3 fusion.6
  39.1 0.0 all-reduce.6.cloned.1.call-update
  39.1 64.1 %all-reduce.4.cloned.1.call-done = f32[64,64,64]{2,1,0:T(8,128)} async-done(((f32[64,64,64]{2,1,0:T(8,128)}), f32[64,64,64]{2,1,0:T(8,128)}) %all-reduce.4.cloned.1.call-update) | async-done | bytes 1048592 | tf_op jit(solution)/shard_map/psum | solution.py:27
  103.3 78.1 %reduce-scatter.2.cloned.1.call-done = f32[64,64,32]{1,2,0:T(8,128)} async-done(((f32[64,64,128]{1,2,0:T(8,128)}), f32[64,64,32]{1,2,0:T(8,128)}) %reduce-scatter.2.cloned.1.call-update) | async-done | bytes 524304 | tf_op jit(solution)/shard_map/reduce_scatter | solution.py:31
  181.4 4.2 %multiply_reduce_fusion = (f32[64]{0:T(128)S(1)}, f32[64,32,64]{2,1,0:T(8,128)S(1)}) fusion(f32[64,64,32]{1,2,0:T(8,128)} %reduce-scatter.2.cloned.1.call-done, f32[64,64,64]{2,1,0:T(8,128)} %all-reduce.4.cloned.1.call-done), kind=kOutput, calls=%fused_computation.3 | convolution fusion | flops 100925376 | bytes 2097408 | tf_op jit(solution)/shard_map/esk,esr->ekr/dot_general | solution.py:32
  185.6 0.4 reshape.6
  186.0 53.9 %all-reduce.6.cloned.1.call-done = f32[64,2048]{1,0:T(8,128)} async-done(((f32[64,2048]{1,0:T(8,128)}), f32[64,2048]{1,0:T(8,128)}) %all-reduce.6.cloned.1.call-update) | async-done | bytes 524304 | tf_op jit(solution)/shard_map/psum | solution.py:42
  239.9 1.6 fusion.1
  241.5 19.3 %all-reduce = (f32[64,64]{1,0:T(8,128)S(1)}, f32[64]{0:T(128)S(1)}) all-reduce(f32[64,64]{1,0:T(8,128)S(1)} %fusion.1, f32[64]{0:T(128)S(1)} %get-tuple-element.7), channel_id=1, replica_groups=mesh['ex'=8,'feat'=4] {'feat'}, use_global_device_ids=true, to_apply=%region_5.6 | all-reduce | flops 4160 | bytes 33280 | tf_op jit(solution)/shard_map/psum | solution.py:47
  260.8 0.7 broadcast_multiply_fusion
  (3 shorter events, 0.0 us)
Async XLA Ops:
  6.5 7.5 %copy-start = (bf16[1024,128]{1,0:T(8,128)(2,1)S(1)}, bf16[1024,128]{1,0:T(8,128)(2,1)}, u32[]{:S(2)}) copy-start(bf16[1024,128]{1,0:T(8,128)(2,1)} %param.11) | copy-start | bytes 786436
  6.5 96.7 %all-reduce.4.cloned.1.call-start = ((), (), s32[]{:S(2)}) async-start(), calls=%async_computation.2 | async-start | bytes 4194304 | tf_op jit(solution)/shard_map/psum | solution.py:27
  14.0 9.6 %copy-start.1 = (f32[32,2048]{1,0:T(8,128)S(1)}, f32[32,2048]{1,0:T(8,128)}, u32[]{:S(2)}) copy-start(f32[32,2048]{1,0:T(8,128)} %param.12) | copy-start | bytes 786436
  14.0 23.8 %copy-start.2 = (s32[32]{0:T(128)S(1)}, s32[32]{0:T(128)}, u32[]{:S(2)}) copy-start(s32[32]{0:T(128)} %param.13) | copy-start | bytes 388
  14.0 167.4 %reduce-scatter.2.cloned.1.call-start = ((), (), s32[]{:S(2)}) async-start(), calls=%async_computation.1 | async-start | bytes 5242880 | tf_op jit(solution)/shard_map/reduce_scatter | solution.py:31
  23.6 216.3 %all-reduce.6.cloned.1.call-start = ((), (), s32[]{:S(2)}) async-start(), calls=%async_computation.3 | async-start | bytes 1048576 | tf_op jit(solution)/shard_map/psum | solution.py:42
Sparse Core Ops, SparseCore 0:
  14.1 89.1 all-reduce.3
  105.6 75.8 reduce-scatter.1
  184.5 55.3 all-reduce.5
where the time goes:
time: 268 us
  waiting for transfers between devices  196 us (73%)
  blocking collectives  33.3 us (12%)
  matrix products  23.9 us (9%)
  between operations  13.2 us (5%)
    reduce_scatter x1, waiting for transfers between devices, shards(): lax.psum_scatter(out_part, 'feat', scatter_dimension=2, tiled=True)  78.1 us
    psum x1, waiting for transfers between devices, shards(): rank_side = lax.psum(rank_part, 'feat')  64.1 us
    psum x1, waiting for transfers between devices, shards(): lax.psum(lang_part, 'ex')  53.9 us
    psum x1, blocking collectives, shards(): inner, squares = lax.psum((inner_part, square_part), 'feat')  19.3 us
    psum x1, blocking collectives, shards(): lax.psum(jnp.sum(heldout_gradient_features * heldout_gradient_features, a...  14.1 us
    dot_general x1, matrix products, shards(): jnp.einsum('esd,dk->esk', output_gradient_rows, output_side_sketch, prefe...  9.45 us
    dot_general x1, matrix products, shards(): jnp.einsum('esd,dr->esr', activations, down_projection_name, preferred_el...  7.42 us
  transfers between devices with their start and end apart: 3, of which 3 were waited for; matrix products, arithmetic and copies ran while one was open for 6% of the time, Pallas kernels for 0%

commit v1 on v0

--- a/solution.py
+++ b/solution.py
@@ -24,7 +24,11 @@
     rank_part = jnp.einsum(
         "esd,dr->esr", activations, down_projection_name, preferred_element_type=jnp.float32
     )
-    rank_side = lax.psum(rank_part, "feat")
+    rank_side = rank_part
+    for hop in (1, 2):
+        rank_side = rank_side + lax.ppermute(
+            rank_side, "feat", [(dev, dev ^ hop) for dev in range(4)]
+        )
     out_part = jnp.einsum(
         "esd,dk->esk", output_gradient_rows, output_side_sketch, preferred_element_type=jnp.float32
     )

time: 268 us -> 322 us (1.20)
  blocking collectives: 33.3 us -> 70.6 us
  waiting for transfers between devices: 196 us -> 202 us
    ppermute x0 -> x2, waiting for transfers between devices: none -> 152 us  [shards(): lax.ppermute(rank_side, 'feat', [(dev, dev ^ hop) for dev in range(4)])]
    reduce_scatter x1, waiting for transfers between devices: 78.1 us -> 0.01 us  [shards(): lax.psum_scatter(out_part, 'feat', scatter_dimension=2, tiled=True)]
    psum x1 -> x0, waiting for transfers between devices: 64.1 us -> none  [shards(): rank_side = lax.psum(rank_part, 'feat')]
    psum x1, blocking collectives: 14.1 us -> 51.3 us  [shards(): lax.psum(jnp.sum(heldout_gradient_features * heldout_gradient_features, a...]
    psum x1, waiting for transfers between devices: 53.9 us -> 50.1 us  [shards(): lax.psum(lang_part, 'ex')]
  transfers between devices with their start and end apart: 3 -> 4, of which waited for: 3 -> 3; matrix products, arithmetic and copies ran while one was open for 6% -> 5% of each run, Pallas kernels for 0% -> 0%
where the time goes in v1:
time: 322 us
  waiting for transfers between devices  202 us (63%)
  blocking collectives  70.6 us (22%)
  matrix products  25.4 us (8%)
  between operations  14.9 us (5%)
  starting transfers between devices  3.23 us (1%)
    ppermute x2, waiting for transfers between devices, shards(): lax.ppermute(rank_side, 'feat', [(dev, dev ^ hop) for dev in range(4)])  152 us
    psum x1, blocking collectives, shards(): lax.psum(jnp.sum(heldout_gradient_features * heldout_gradient_features, a...  51.3 us
    psum x1, waiting for transfers between devices, shards(): lax.psum(lang_part, 'ex')  50.1 us
    psum x1, blocking collectives, shards(): inner, squares = lax.psum((inner_part, square_part), 'feat')  19.3 us
    dot_general x1, matrix products, shards(): jnp.einsum('esd,dk->esk', output_gradient_rows, output_side_sketch, prefe...  9.44 us
    dot_general x1, matrix products, shards(): jnp.einsum('esd,dr->esr', activations, down_projection_name, preferred_el...  7.58 us
  transfers between devices with their start and end apart: 4, of which 3 were waited for; matrix products, arithmetic and copies ran while one was open for 5% of the time, Pallas kernels for 0%

profile of v1, /device:TPU:0, one launch (start us, length us, event | category | flops | bytes accessed | tf_op | source)
XLA Modules:
  0.0 321.6 jit_solution(12498878128094886975)
XLA Ops:
  7.4 0.0 copy-start
  7.4 0.0 reduce-scatter.2.cloned.1.call-start
  7.4 0.9 copy-done
  8.3 9.4 %fusion.5 = f32[64,64,128]{1,2,0:T(8,128)} fusion(bf16[64,64,1024]{2,1,0:T(8,128)(2,1)} %param.8, bf16[1024,128]{1,0:T(8,128)(2,1)S(1)} %copy-done), kind=kOutput, calls=%fused_computation.8 | convolution fusion | flops 1073741824 | bytes 10747904 | tf_op jit(solution)/shard_map/esd,dk->esk/dot_general | solution.py:32
  17.8 0.0 copy-start.3
  17.8 0.0 copy-start.4
  17.8 0.0 reduce-scatter.2.cloned.1.call-update
  17.8 0.0 all-reduce.3.cloned.1.call-start
  17.8 0.9 copy-done.3
  18.7 0.0 copy-done.4
  18.7 7.6 %convolution_bitcast_fusion = f32[64,64,64]{1,2,0:T(8,128)S(1)} fusion(bf16[64,64,1024]{2,1,0:T(8,128)(2,1)} %param.7, bf16[1024,128]{1,0:T(8,128)(2,1)S(1)} %copy-done.3, bf16[128,64]{0,1:T(8,128)(2,1)S(1)} %copy-done.4), kind=kOutput, calls=%fused_computation.2 | convolution fusion | flops 553713664 | bytes 9715712 | tf_op jit(solution)/shard_map/esd,dr->esr/dot_general | solution.py:24
  26.3 0.0 copy-start.1
  26.3 0.0 copy-start.2
  26.3 0.0 copy-start.5
  26.3 3.1 collective-permute-start
  29.4 0.0 copy-done.1
  29.4 111.5 %collective-permute-done = f32[64,64,64]{1,2,0:T(8,128)S(1)} collective-permute-done((f32[64,64,64]{1,2,0:T(8,128)S(1)}, f32[64,64,64]{1,2,0:T(8,128)S(1)}, u32[]{:S(2)}, u32[]{:S(2)}) %collective-permute-start) | collective-permute-done | bytes 1048608 | tf_op jit(solution)/shard_map/ppermute | solution.py:29
  141.0 2.1 add.34
  143.0 0.1 collective-permute-start.1
  143.1 0.0 copy-done.2
  143.1 0.1 multiply_reduce_fusion.1
  143.2 51.3 %psum.28 = f32[32]{0:T(128)S(1)} all-reduce(f32[32]{0:T(128)S(1)} %multiply_reduce_fusion.1), channel_id=1, replica_groups=mesh['ex'=8,'feat'=4] {'feat'}, use_global_device_ids=true, to_apply=%region_2.0 | all-reduce | flops 32 | bytes 256 | tf_op jit(solution)/shard_map/psum | solution.py:39
  194.6 0.0 copy-done.5
  194.6 1.3 fusion.8
  195.9 0.0 all-reduce.3.cloned.1.call-update
  195.9 40.7 %collective-permute-done.1 = f32[64,64,64]{1,2,0:T(8,128)} collective-permute-done((f32[64,64,64]{1,2,0:T(8,128)S(1)}, f32[64,64,64]{1,2,0:T(8,128)}, u32[]{:S(2)}, u32[]{:S(2)}) %collective-permute-start.1) | collective-permute-done | bytes 1048608 | tf_op jit(solution)/shard_map/ppermute | solution.py:29
  236.6 0.0 reduce-scatter.2.cloned.1.call-done
  236.6 5.5 %multiply_reduce_fusion = (f32[64]{0:T(128)S(1)}, f32[64,32,64]{2,1,0:T(8,128)S(1)}) fusion(f32[64,64,32]{1,2,0:T(8,128)} %reduce-scatter.2.cloned.1.call-done, f32[64,64,64]{1,2,0:T(8,128)S(1)} %add.34, f32[64,64,64]{1,2,0:T(8,128)} %collective-permute-done.1), kind=kOutput, calls=%fused_computation.5 | convolution fusion | flops 101187520 | bytes 3145984 | tf_op jit(solution)/shard_map/esk,esr->ekr/dot_general | solution.py:36
  242.0 0.4 reshape.6
  242.4 50.1 %all-reduce.3.cloned.1.call-done = f32[64,2048]{1,0:T(8,128)} async-done(((f32[64,2048]{1,0:T(8,128)}), f32[64,2048]{1,0:T(8,128)}) %all-reduce.3.cloned.1.call-update) | async-done | bytes 524304 | tf_op jit(solution)/shard_map/psum | solution.py:46
  292.5 1.6 fusion.3
  294.1 19.3 %all-reduce = (f32[64,64]{1,0:T(8,128)S(1)}, f32[64]{0:T(128)S(1)}) all-reduce(f32[64,64]{1,0:T(8,128)S(1)} %fusion.3, f32[64]{0:T(128)S(1)} %get-tuple-element.7), channel_id=1, replica_groups=mesh['ex'=8,'feat'=4] {'feat'}, use_global_device_ids=true, to_apply=%region_4.5 | all-reduce | flops 4160 | bytes 33280 | tf_op jit(solution)/shard_map/psum | solution.py:51
  313.4 0.7 broadcast_multiply_fusion
  (3 shorter events, 0.0 us)
Async XLA Ops:
  7.4 1.0 copy-start
  7.4 229.2 %reduce-scatter.2.cloned.1.call-start = ((), (), s32[]{:S(2)}) async-start(), calls=%async_computation.1 | async-start | bytes 5242880 | tf_op jit(solution)/shard_map/reduce_scatter | solution.py:35
  17.8 0.9 copy-start.3
  17.8 1.0 copy-start.4
  17.8 274.7 %all-reduce.3.cloned.1.call-start = ((), (), s32[]{:S(2)}) async-start(), calls=%async_computation.2 | async-start | bytes 1048576 | tf_op jit(solution)/shard_map/psum | solution.py:46
  26.3 3.2 copy-start.1
  26.3 116.8 %copy-start.2 = (f32[32,2048]{1,0:T(8,128)S(1)}, f32[32,2048]{1,0:T(8,128)}, u32[]{:S(2)}) copy-start(f32[32,2048]{1,0:T(8,128)} %param.12) | copy-start | bytes 786436
  26.3 168.3 %copy-start.5 = (s32[32]{0:T(128)S(1)}, s32[32]{0:T(128)}, u32[]{:S(2)}) copy-start(s32[32]{0:T(128)} %param.13) | copy-start | bytes 388
  26.3 114.6 %collective-permute-start = (f32[64,64,64]{1,2,0:T(8,128)S(1)}, f32[64,64,64]{1,2,0:T(8,128)S(1)}, u32[]{:S(2)}, u32[]{:S(2)}) collective-permute-start(f32[64,64,64]{1,2,0:T(8,128)S(1)} %convolution_bitcast_fusion), channel_id=1, source_target_pairs={{0,1},{1,0},{2,3},{3,2},{4,5},{5,4},{6,7},{7,6},{8,9},{9,8},{10,11... | collective-permute-start | bytes 3145736 | tf_op jit(solution)/shard_map/ppermute | solution.py:29
  143.0 93.5 %collective-permute-start.1 = (f32[64,64,64]{1,2,0:T(8,128)S(1)}, f32[64,64,64]{1,2,0:T(8,128)}, u32[]{:S(2)}, u32[]{:S(2)}) collective-permute-start(f32[64,64,64]{1,2,0:T(8,128)S(1)} %add.34), channel_id=1, source_target_pairs={{0,2},{1,3},{2,0},{3,1},{4,6},{5,7},{6,4},{7,5},{8,10},{9,11},{10,... | collective-permute-start | bytes 3145736 | tf_op jit(solution)/shard_map/ppermute | solution.py:29
Sparse Core Ops, SparseCore 0:
  17.9 123.8 reduce-scatter.1
Sparse Core Ops, SparseCore 1:
  196.0 96.5 all-reduce.2
